TPU v7x, 32 devices: a whole 2x2x4 slice. The times are simulated.
32 devices in a mesh: row: 4 (over z), col: 8 (over y, x, core).
Axes of the slice: x: 2, y: 2, z: 4, core: 2. Of those that a mesh axis runs over, the one named last changes fastest.
Arguments:
- hidden: bfloat16 [4096, 2048], P(('row', 'col')), may hold values from -6 to 6
- cached_lengths: int32 [4], replicated, may hold values from 1024 to 4096, as said below
- request_order: int32 [4], replicated, may hold values from 0 to 3, each once
- cache_keys: bfloat16 [4, 4096, 2048], P('row', None, 'col'), may hold values from -480 to 480
- cache_values: bfloat16 [4, 4096, 2048], P('row', None, 'col'), may hold values from -6 to 6
- attn_gain: bfloat16 [2048], replicated, may hold values from 0.5 to 1.5
- w_qkv: bfloat16 [2048, 16, 384], P(None, 'col'), may hold values from -0.125 to 0.125
- w_out: bfloat16 [2048, 2048], P('col'), may hold values from -0.125 to 0.125
- moe_gain: bfloat16 [2048], replicated, may hold values from 0.5 to 1.5
- expert_ids: int32 [4096, 6], P(('row', 'col')), may hold values from 0 to 63, all different within a row; in each aligned block of 128 rows (0 to 127, 128 to 255, ...) at most 16 rows name the same one
- gate_weights: bfloat16 [4096, 6], P(('row', 'col')), may hold values from 0.049804688 to 0.3984375
- w_in: bfloat16 [128, 2048, 1408], P(('row', 'col')), may hold values from -0.125 to 0.125
- w_down: bfloat16 [128, 704, 2048], P(('row', 'col')), may hold values from -0.15625 to 0.15625
Outputs:
- new_hidden: bfloat16 [4096, 2048], P(('row', 'col'))
- new_keys: bfloat16 [4096, 2048], P('row', 'col')
- new_values: bfloat16 [4096, 2048], P('row', 'col')
Inputs may be any that keep to these rules, and one draw needn't show every extreme that they name: `cached_lengths`: every request has at least a quarter of 4096 cached tokens, and some request has exactly 4096. `request_order`: each slot serves a different request. `expert_ids`: among the rows of one device (aligned blocks of 128 tokens) no expert is named by more than 16 rows, a bound that some block reaches.
All inputs are finite; a program needn't handle non-finite values.
Results may differ from a plain program's by a relative error of at most 0.015.
Values may be sent and summed in bfloat16 or wider, within the bound.
No kernel may reach another device: no remote copies, remote signals or barrier semaphores. Data moves between devices by JAX's collectives and lax.ppermute only.
A program may use at most 192 MiB of HBM per device.

v0:
```python
import jax
import jax.numpy as jnp
from jax import lax
from jax.sharding import PartitionSpec as P

EXPERTS = 64
WINDOW = 4096
SINKS = 4
CAP = 16
EPS = 1e-06
THETA = 10000.0


def rms_scale(matrix, scaling):
    values = matrix.astype(jnp.float32)
    factor = lax.rsqrt(jnp.mean(values * values, axis=-1, keepdims=True) + EPS)
    return values * factor * scaling.astype(jnp.float32)


def rotate(vectors, positions):
    half_width = vectors.shape[-1] // 2
    frequency = THETA ** (-2.0 * jnp.arange(half_width, dtype=jnp.float32) / vectors.shape[-1])
    angles = positions.astype(jnp.float32)[..., None] * frequency
    cosine = jnp.cos(angles)[..., None, :]
    sine_part = jnp.sin(angles)[..., None, :]
    leading = vectors[..., :half_width]
    trailing = vectors[..., half_width:]
    return jnp.concatenate(
        [leading * cosine - trailing * sine_part, trailing * cosine + leading * sine_part], axis=-1
    )


def attend(queries, key_rows, value_rows, key_places, key_valid, query_places):
    scores = jnp.einsum(
        "nhe,mhe->hnm", queries, key_rows, preferred_element_type=jnp.float32
    ) * queries.shape[-1] ** (-0.5)
    distance = query_places[:, None] - key_places[None, :]
    allowed = (
        key_valid[None, :] & (distance >= 0) & ((distance < WINDOW) | (key_places[None, :] < SINKS))
    )
    scores = jnp.where(allowed[None], scores, -1e30)
    highest = jnp.max(scores, axis=-1, keepdims=True)
    weights = jnp.exp(scores - highest)
    shares = (weights / jnp.sum(weights, axis=-1, keepdims=True)).astype(jnp.bfloat16)
    return jnp.einsum(
        "hnm,mhe->nhe", shares, value_rows, preferred_element_type=jnp.float32
    ).astype(jnp.bfloat16)


def body(
    hidden,
    cached_lengths,
    request_order,
    cache_keys,
    cache_values,
    attn_gain,
    w_qkv,
    w_out,
    moe_gain,
    expert_ids,
    gate_weights,
    w_in,
    w_down,
):
    tok_rows, model_width = hidden.shape
    heads_here = w_qkv.shape[1]
    head_width = w_qkv.shape[2] // 3
    normed = rms_scale(hidden, attn_gain).astype(jnp.bfloat16)
    qkv_matrix = w_qkv.reshape(model_width, heads_here * 3 * head_width)
    projected = jnp.dot(
        lax.all_gather(normed, "col", axis=0, tiled=True),
        qkv_matrix,
        preferred_element_type=jnp.float32,
    )
    new_rows = projected.shape[0]
    projected = projected.reshape(new_rows, heads_here, 3, head_width)
    row_index = lax.axis_index("row")
    places = jnp.arange(request_order.shape[0], dtype=jnp.int32)
    request = jnp.sum(jnp.where(places == row_index, request_order, 0))
    length = jnp.sum(jnp.where(places == request, cached_lengths, 0))
    query_pos = length + jnp.arange(new_rows, dtype=jnp.int32)
    queries = rotate(projected[:, :, 0], query_pos).astype(jnp.bfloat16)
    fresh_keys = rotate(projected[:, :, 1], query_pos).astype(jnp.bfloat16)
    fresh_values = projected[:, :, 2].astype(jnp.bfloat16)
    cache_rows = cache_keys.shape[1]
    cache_places = jnp.arange(cache_rows, dtype=jnp.int32)
    keys_all = jnp.concatenate(
        [cache_keys[0].reshape(cache_rows, heads_here, head_width), fresh_keys], axis=0
    )
    values_all = jnp.concatenate(
        [cache_values[0].reshape(cache_rows, heads_here, head_width), fresh_values], axis=0
    )
    key_places = jnp.concatenate([cache_places, query_pos])
    key_valid = jnp.concatenate([cache_places < length, jnp.ones((new_rows,), jnp.bool_)])
    block_rows = min(512, new_rows)
    query_blocks = queries.reshape(new_rows // block_rows, block_rows, heads_here, head_width)
    position_blocks = query_pos.reshape(new_rows // block_rows, block_rows)

    def one_block(operands):
        block_queries, block_places = operands
        return attend(block_queries, keys_all, values_all, key_places, key_valid, block_places)

    context = lax.map(one_block, (query_blocks, position_blocks)).reshape(
        new_rows, heads_here * head_width
    )
    attention = lax.psum_scatter(
        jnp.dot(context, w_out, preferred_element_type=jnp.float32).astype(jnp.bfloat16),
        "col",
        scatter_dimension=0,
        tiled=True,
    ).astype(jnp.float32)
    residual = hidden.astype(jnp.float32) + attention
    moe_in = rms_scale(residual, moe_gain).astype(jnp.bfloat16)
    top_count = expert_ids.shape[1]
    flat_ids = expert_ids.reshape(-1)
    onehot = (flat_ids[:, None] == jnp.arange(EXPERTS, dtype=jnp.int32)[None, :]).astype(jnp.int32)
    slot_rank = jnp.sum((jnp.cumsum(onehot, axis=0) - onehot) * onehot, axis=1)
    slot_index = flat_ids * CAP + slot_rank
    owners = jnp.arange(flat_ids.shape[0], dtype=jnp.int32) // top_count
    slot_table = jnp.full((EXPERTS * CAP,), tok_rows, jnp.int32).at[slot_index].set(owners)
    padded = jnp.concatenate([moe_in, jnp.zeros((1, model_width), jnp.bfloat16)], axis=0)
    routed_rows = padded[slot_table]
    row_count = lax.axis_size("row")
    col_count = lax.axis_size("col")
    device_count = row_count * col_count
    per_device = w_in.shape[0]
    half_units = w_down.shape[1]
    outgoing = routed_rows.reshape(EXPERTS, 1, CAP, model_width)
    outgoing = jnp.broadcast_to(outgoing, (EXPERTS, 2, CAP, model_width))
    sending = outgoing.reshape(device_count, per_device, CAP, model_width)
    both_parts = jnp.einsum(
        "shcd,hdf->shcf",
        lax.all_to_all(sending, ("row", "col"), split_axis=0, concat_axis=0, tiled=True),
        w_in,
        preferred_element_type=jnp.float32,
    )
    activated = (jax.nn.silu(both_parts[..., :half_units]) * both_parts[..., half_units:]).astype(
        jnp.bfloat16
    )
    results = jnp.einsum("shcf,hfd->shcd", activated, w_down, preferred_element_type=jnp.float32)
    returned = lax.all_to_all(
        results.astype(jnp.bfloat16), ("row", "col"), split_axis=0, concat_axis=0, tiled=True
    ).astype(results.dtype)
    flat_returned = returned.reshape(EXPERTS * 2 * CAP, model_width)
    half_ids = jnp.arange(2, dtype=jnp.int32)
    gather_index = (flat_ids[:, None] * 2 + half_ids[None, :]) * CAP + slot_rank[:, None]
    picked = flat_returned[gather_index.reshape(-1)].reshape(tok_rows, top_count, 2, model_width)
    part_rows = (picked[:, :, 0] + picked[:, :, 1]).astype(jnp.bfloat16)
    expert_sum = jnp.einsum(
        "tk,tkd->td", gate_weights, part_rows, preferred_element_type=jnp.float32
    )
    new_hidden = (residual + expert_sum).astype(jnp.bfloat16)
    new_keys = fresh_keys.reshape(new_rows, heads_here * head_width)
    new_values = fresh_values.reshape(new_rows, heads_here * head_width)
    return (new_hidden, new_keys, new_values)


def solution(mesh):
    in_specs = (
        P(("row", "col"), None),
        P(),
        P(),
        P("row", None, "col"),
        P("row", None, "col"),
        P(),
        P(None, "col", None),
        P("col", None),
        P(),
        P(("row", "col"), None),
        P(("row", "col"), None),
        P(("row", "col"), None, None),
        P(("row", "col"), None, None),
    )
    out_specs = (P(("row", "col"), None), P("row", "col"), P("row", "col"))
    return jax.shard_map(body, mesh=mesh, in_specs=in_specs, out_specs=out_specs, check_vma=False)
```

profile of v0, /device:TPU:0, one launch (start us, length us, event | category | flops | bytes accessed | tf_op | source)
XLA Modules:
  0.0 759.5 jit_solution(14790934212152108399)
XLA Ops:
  22.7 4.7 copy.43
  33.3 17.6 %all-gather.2.cloned.1.call-done = bf16[1024,2048]{1,0:T(8,128)(2,1)} async-done(((bf16[128,2048]{1,0:T(8,128)(2,1)}), bf16[1024,2048]{1,0:T(8,128)(2,1)}) %all-gather.2.cloned.1.call-update) | async-done | bytes 4194320 | tf_op jit(solution)/shard_map/all_gather | solution.py:71
  50.9 6.2 fusion.31
  78.7 4.4 copy.49
  84.6 102.0 %while.10 = (s32[]{:T(128)}, bf16[2,512,2,128]{3,2,1,0:T(2,128)(2,1)}, pred[5120]{0:T(1024)(128)(4,1)S(1)}, s32[2,512]{1,0:T(2,128)S(1)}, s32[5120]{0:T(1024)S(1...) while((s32[]{:T(128)}, ...), condition=%wide.region_6.7_spmd, body=%wide.region_3.6_spmd.sunk | while | flops 2742167552 | bytes 99685544 | solution.py:103
  88.7 10.3 %fusion.77 = f32[2,512,5120]{2,1,0:T(8,128)} fusion(bf16[5120,2,128]{2,0,1:T(8,128)(2,1)} %get-tuple-element.178, bf16[2,512,2,128]{3,1,2,0:T(8,128)(2,1)S(1)} %get-tuple-element.177, s32[]{:T(128)S(6)} %copy.103), kind=kOutput, calls=%fused_computation.20.clone.1 | convolution fusion | flops 1342177280 | bytes 23855108 | tf_op jit(solution)/shard_map/while/body/eval_jaxpr/nhe,mhe->hnm/dot_general | solution.py:34
  99.1 25.0 %fusion.79 = (f32[2,512]{1,0:T(2,128)S(1)}, f32[2,512,5120]{2,1,0:T(8,128)}) fusion(f32[2,512,5120]{2,1,0:T(8,128)} %fusion.77, pred[512,5120]{1,0:T(8,128)(4,1)S(1)} %fusion.78), kind=kOutput, calls=%fused_computation.113.clone.1 | output fusion | flops 31462400 | bytes 44568576 | tf_op jit(solution)/shard_map/while/body/eval_jaxpr/sub | solution.py:43
  124.1 10.7 %fusion.80 = bf16[1,512,2,128]{3,1,2,0:T(8,128)(2,1)S(1)} fusion(bf16[5120,2,128]{2,0,1:T(8,128)(2,1)} %get-tuple-element.179, f32[2,512,5120]{2,1,0:T(8,128)} %get-tuple-element.152, f32[2,512]{1,0:T(2,128)S(1)} %get-tuple-element.153), kind=kOutput, calls=%fused_computation.18.clone.1 | convolution fusion | flops 1352794112 | bytes 23859200 | tf_op jit(solution)/shard_map/while/body/eval_jaxpr/hnm,mhe->nhe/dot_general | solution.py:45
  139.5 10.3 %fusion.77 = f32[2,512,5120]{2,1,0:T(8,128)} fusion(bf16[5120,2,128]{2,0,1:T(8,128)(2,1)} %get-tuple-element.178, bf16[2,512,2,128]{3,1,2,0:T(8,128)(2,1)S(1)} %get-tuple-element.177, s32[]{:T(128)S(6)} %copy.103), kind=kOutput, calls=%fused_computation.20.clone.1 | convolution fusion | flops 1342177280 | bytes 23855108 | tf_op jit(solution)/shard_map/while/body/eval_jaxpr/nhe,mhe->hnm/dot_general | solution.py:34
  149.8 25.0 %fusion.79 = (f32[2,512]{1,0:T(2,128)S(1)}, f32[2,512,5120]{2,1,0:T(8,128)}) fusion(f32[2,512,5120]{2,1,0:T(8,128)} %fusion.77, pred[512,5120]{1,0:T(8,128)(4,1)S(1)} %fusion.78), kind=kOutput, calls=%fused_computation.113.clone.1 | output fusion | flops 31462400 | bytes 44568576 | tf_op jit(solution)/shard_map/while/body/eval_jaxpr/sub | solution.py:43
  174.8 10.7 %fusion.80 = bf16[1,512,2,128]{3,1,2,0:T(8,128)(2,1)S(1)} fusion(bf16[5120,2,128]{2,0,1:T(8,128)(2,1)} %get-tuple-element.179, f32[2,512,5120]{2,1,0:T(8,128)} %get-tuple-element.152, f32[2,512]{1,0:T(2,128)S(1)} %get-tuple-element.153), kind=kOutput, calls=%fused_computation.18.clone.1 | convolution fusion | flops 1352794112 | bytes 23859200 | tf_op jit(solution)/shard_map/while/body/eval_jaxpr/hnm,mhe->nhe/dot_general | solution.py:45
  197.5 44.9 %reduce-scatter.2.cloned.1.call-done = bf16[128,2048]{1,0:T(8,128)(2,1)} async-done(((bf16[1024,2048]{1,0:T(8,128)(2,1)}), bf16[128,2048]{1,0:T(8,128)(2,1)}) %reduce-scatter.2.cloned.1.call-update) | async-done | bytes 524304 | tf_op jit(solution)/shard_map/reduce_scatter | solution.py:106
  245.0 6.1 gather_fusion
  251.1 6.8 broadcast_in_dim.43
  257.8 188.2 %all_to_all.10 = bf16[32,4,16,2048]{3,2,1,0:T(8,128)(2,1)} all-to-all(bf16[32,4,16,2048]{3,2,1,0:T(8,128)(2,1)} %bitcast.105), channel_id=1, replica_groups=mesh['row'=4,'col'=8] {'row','col'}, dimensions={0} | all-to-all | bytes 16777216 | tf_op jit(solution)/shard_map/all_to_all | solution.py:133
  446.1 21.2 %fusion.22 = f32[32,4,16,1408]{3,2,0,1:T(8,128)} fusion(bf16[4,2048,1408]{2,1,0:T(8,128)(2,1)} %param.26, bf16[32,4,16,2048]{3,2,1,0:T(8,128)(2,1)} %all_to_all.10), kind=kOutput, calls=%fused_computation.35 | convolution fusion | flops 11811160064 | bytes 42991616 | tf_op jit(solution)/shard_map/shcd,hdf->shcf/dot_general | solution.py:131
  467.2 15.5 %convert_bitcast_fusion = bf16[32,4,16,2048]{3,2,0,1:T(8,128)(2,1)} fusion(bf16[4,704,2048]{2,1,0:T(8,128)(2,1)} %param.27, f32[32,4,16,1408]{3,2,0,1:T(8,128)} %fusion.22), kind=kOutput, calls=%fused_computation.34 | convolution fusion | flops 5918425088 | bytes 32505856 | tf_op jit(solution)/shard_map/shcf,hfd->shcd/dot_general | solution.py:140
  482.7 8.3 %copy.57 = bf16[32,4,16,2048]{3,2,1,0:T(8,128)(2,1)} copy(bf16[32,4,16,2048]{3,2,0,1:T(8,128)(2,1)} %convert_bitcast_fusion) | data formatting | bytes 16777216 | tf_op jit(solution)/shard_map/convert_element_type | solution.py:142
  499.0 182.0 %all-to-all-done.1 = bf16[32,4,16,2048]{3,2,1,0:T(8,128)(2,1)} async-done(((bf16[32,4,16,2048]{3,2,1,0:T(8,128)(2,1)}), bf16[32,4,16,2048]{3,2,1,0:T(8,128)(2,1)}, u32[]{:S(2)}, u32[]{:S(2)}) %all-to-all-start.1) | async-done | bytes 8388640 | tf_op jit(solution)/shard_map/all_to_all | solution.py:141
  681.0 11.2 %bitcast_convert_fusion = f32[2048,2048]{1,0:T(8,128)} fusion(bf16[32,4,16,2048]{3,2,1,0:T(8,128)(2,1)} %all-to-all-done.1), kind=kLoop, calls=%fused_computation.32 | loop fusion | flops 4194304 | bytes 25165824 | tf_op jit(solution)/shard_map/reshape | solution.py:144
  692.3 18.3 %gather_fusion.1 = f32[1536,2048]{1,0:T(8,128)} fusion(f32[2048,2048]{1,0:T(8,128)} %bitcast_convert_fusion, s32[2048]{0:T(1024)S(1)} %pad_clamp_fusion), kind=kCustom, calls=%fused_computation.1 | custom fusion | bytes 25171968 | tf_op jit(solution)/shard_map/gather | solution.py:147
  710.5 15.3 %reshape.296 = f32[128,6,2,2048]{3,2,1,0:T(2,128)} reshape(f32[1536,2048]{1,0:T(8,128)} %gather_fusion.1) | data formatting | bytes 25165824 | tf_op jit(solution)/shard_map/reshape | solution.py:147
  725.8 15.6 %fusion.61 = (f32[128,6,1,2048]{3,2,1,0:T(1,128)S(1)}, f32[128,6,1,2048]{3,2,1,0:T(1,128)S(1)}) fusion(f32[128,6,2,2048]{3,2,1,0:T(2,128)} %reshape.296), kind=kLoop, calls=%fused_computation.114 | loop fusion | bytes 25165824 | tf_op jit(solution)/shard_map/slice | solution.py:148
  741.4 7.2 fusion.35
  (108 shorter events, 79.0 us)
Async XLA Ops:
  7.2 179.4 %copy-start = (bf16[256,2048]{1,0:T(8,128)(2,1)S(1)}, bf16[256,2048]{1,0:T(8,128)(2,1)}, u32[]{:S(2)}) copy-start(bf16[256,2048]{1,0:T(8,128)(2,1)} %param.22) | copy-start | bytes 3145732
  7.2 43.7 %all-gather.2.cloned.1.call-start = ((), (), s32[]{:S(2)}) async-start(), calls=%async_computation.3 | async-start | bytes 4718592 | tf_op jit(solution)/shard_map/all_gather | solution.py:71
  11.3 231.1 %reduce-scatter.2.cloned.1.call-start = ((), (), s32[]{:S(2)}) async-start(), calls=%async_computation.4 | async-start | bytes 4718592 | tf_op jit(solution)/shard_map/reduce_scatter | solution.py:106
  18.4 9.0 %copy-start.12 = (s32[4]{0:T(128)S(1)}, s32[4]{0:T(128)}, u32[]{:S(2)}) copy-start(s32[4]{0:T(128)} %param.17) | copy-start | bytes 52
  18.4 9.6 %copy-start.13 = (s32[4]{0:T(128)S(1)}, s32[4]{0:T(128)}, u32[]{:S(2)}) copy-start(s32[4]{0:T(128)} %param.16) | copy-start | bytes 52
  57.1 1.7 copy-start.6
  57.1 3.1 copy-start.2
  76.2 0.8 copy-start.3
  124.1 10.7 %copy-start.7 = (bf16[2,512,2,128]{3,2,1,0:T(2,128)(2,1)S(1)}, bf16[2,512,2,128]{3,2,1,0:T(2,128)(2,1)}, u32[]{:S(2)}) copy-start(bf16[2,512,2,128]{3,2,1,0:T(2,128)(2,1)} %get-tuple-element.164) | copy-start | bytes 1572868 | tf_op jit(solution)/shard_map/while
  135.1 0.8 copy-start.8
  174.8 10.7 %copy-start.7 = (bf16[2,512,2,128]{3,2,1,0:T(2,128)(2,1)S(1)}, bf16[2,512,2,128]{3,2,1,0:T(2,128)(2,1)}, u32[]{:S(2)}) copy-start(bf16[2,512,2,128]{3,2,1,0:T(2,128)(2,1)} %get-tuple-element.164) | copy-start | bytes 1572868 | tf_op jit(solution)/shard_map/while
  185.8 0.8 copy-start.8
  186.6 4.3 copy-start.9
  186.6 4.7 copy-start.10
  186.6 55.8 %copy-start.1 = (bf16[128,2048]{1,0:T(8,128)(2,1)S(1)}, bf16[128,2048]{1,0:T(8,128)(2,1)}, u32[]{:S(2)}) copy-start(bf16[128,2048]{1,0:T(8,128)(2,1)} %param.15) | copy-start | bytes 1572868
  491.0 4.0 copy-start.11
  491.0 7.0 copy-start.4
  491.0 190.0 %all-to-all-start.1 = ((bf16[32,4,16,2048]{3,2,1,0:T(8,128)(2,1)}), bf16[32,4,16,2048]{3,2,1,0:T(8,128)(2,1)}, u32[]{:S(2)}, u32[]{:S(2)}) async-start(bf16[32,4,16,2048]{3,2,1,0:T(8,128)(2,1)} %copy.57), calls=%async_computation.2 | async-start | bytes 16777216 | tf_op jit(solution)/shard_map/all_to_all | solution.py:141
  748.6 2.6 copy-start.5
Sparse Core Ops, SparseCore 0:
  11.4 39.4 all-gather.1
  191.0 51.3 reduce-scatter.1
where the time goes:
time: 767 us; the launch traced here: 759 us
  waiting for transfers between devices  245 us (32%)
  blocking collectives  188 us (25%)
  local copies, waits for them, and re-layouts  114 us (15%)
  other arithmetic  102 us (13%)
  matrix products  91.8 us (12%)
  between operations  14.6 us (2%)
    all_to_all x1, blocking collectives, body(): lax.all_to_all(sending, ('row', 'col'), split_axis=0, concat_axis=0, tile...  188 us
    all_to_all x1, waiting for transfers between devices, body(): lax.all_to_all(results.astype(jnp.bfloat16), ('row', 'col'), split_axis=0...  182 us
    sub x2, other arithmetic, attend(): weights = jnp.exp(scores - highest)  49.9 us
    reduce_scatter x1, waiting for transfers between devices, body(): lax.psum_scatter(jnp.dot(context, w_out, preferred_element_type=jnp.float...  44.9 us
    dot_general x2, matrix products, attend(): jnp.einsum('hnm,mhe->nhe', shares, value_rows, preferred_element_type=jnp...  21.4 us
    dot_general x1, matrix products, body(): jnp.einsum('shcd,hdf->shcf', lax.all_to_all(sending, ('row', 'col'), spli...  21.2 us
    dot_general x2, matrix products, attend(): jnp.einsum('nhe,mhe->hnm', queries, key_rows, preferred_element_type=jnp....  20.7 us
    gather x1, local copies, waits for them, and re-layouts, body(): flat_returned[gather_index.reshape(-1)]  18.3 us
  transfers between devices with their start and end apart: 3, of which 3 were waited for; matrix products, arithmetic and copies ran while one was open for 4% of the time, Pallas kernels for 0%

commit v1 on v0

--- a/solution.py
+++ b/solution.py
@@ -9,6 +9,18 @@
 CAP = 16
 EPS = 1e-06
 THETA = 10000.0
+
+
+def gather_by_bits(x, axis, dim):
+    ways, here = (lax.axis_size(axis), lax.axis_index(axis))
+    grown, reach = (x, 1)
+    while reach < ways:
+        theirs = lax.ppermute(grown, axis, [(d, d ^ reach) for d in range(ways)])
+        mine_first = jnp.concatenate([grown, theirs], axis=dim)
+        theirs_first = jnp.concatenate([theirs, grown], axis=dim)
+        grown = jnp.where(here & reach == 0, mine_first, theirs_first)
+        reach = 2 * reach
+    return grown
 
 
 def rms_scale(matrix, scaling):
@@ -68,9 +80,7 @@
     normed = rms_scale(hidden, attn_gain).astype(jnp.bfloat16)
     qkv_matrix = w_qkv.reshape(model_width, heads_here * 3 * head_width)
     projected = jnp.dot(
-        lax.all_gather(normed, "col", axis=0, tiled=True),
-        qkv_matrix,
-        preferred_element_type=jnp.float32,
+        gather_by_bits(normed, "col", 0), qkv_matrix, preferred_element_type=jnp.float32
     )
     new_rows = projected.shape[0]
     projected = projected.reshape(new_rows, heads_here, 3, head_width)

time: 767 us -> 808 us (1.053)
  waiting for transfers between devices: 245 us -> 277 us
    ppermute x0 -> x3, waiting for transfers between devices: none -> 48.9 us  [gather_by_bits(): theirs = lax.ppermute(grown, axis, [(d, d ^ reach) for d in range(ways)])]
    all_gather x1 -> x0, waiting for transfers between devices: 17.6 us -> none  [body(): lax.all_gather(normed, 'col', axis=0, tiled=True)]
  transfers between devices with their start and end apart: 3 -> 5, of which waited for: 3 -> 5; matrix products, arithmetic and copies ran while one was open for 4% -> 4% of each run, Pallas kernels for 0% -> 0%
where the time goes in v1:
time: 808 us; the launch traced here: 799 us
  waiting for transfers between devices  277 us (34%)
  blocking collectives  188 us (23%)
  local copies, waits for them, and re-layouts  114 us (14%)
  other arithmetic  102 us (13%)
  matrix products  93.5 us (12%)
  between operations  14.6 us (2%)
  starting transfers between devices  9.24 us (1%)
    all_to_all x1, blocking collectives, body(): lax.all_to_all(sending, ('row', 'col'), split_axis=0, concat_axis=0, tile...  188 us
    all_to_all x1, waiting for transfers between devices, body(): lax.all_to_all(results.astype(jnp.bfloat16), ('row', 'col'), split_axis=0...  182 us
    sub x2, other arithmetic, attend(): weights = jnp.exp(scores - highest)  49.9 us
    ppermute x3, waiting for transfers between devices, gather_by_bits(): theirs = lax.ppermute(grown, axis, [(d, d ^ reach) for d in range(ways)])  48.9 us
    reduce_scatter x1, waiting for transfers between devices, body(): lax.psum_scatter(jnp.dot(context, w_out, preferred_element_type=jnp.float...  45.9 us
    dot_general x2, matrix products, attend(): jnp.einsum('hnm,mhe->nhe', shares, value_rows, preferred_element_type=jnp...  21.4 us
    dot_general x1, matrix products, body(): jnp.einsum('shcd,hdf->shcf', lax.all_to_all(sending, ('row', 'col'), spli...  21.2 us
    dot_general x2, matrix products, attend(): jnp.einsum('nhe,mhe->hnm', queries, key_rows, preferred_element_type=jnp....  20.7 us
  transfers between devices with their start and end apart: 5, of which 5 were waited for; matrix products, arithmetic and copies ran while one was open for 4% of the time, Pallas kernels for 0%

profile of v1, /device:TPU:0, one launch (start us, length us, event | category | flops | bytes accessed | tf_op | source)
XLA Modules:
  0.0 799.1 jit_solution(9004725853105368397)
XLA Ops:
  15.7 23.5 %collective-permute-done.1 = bf16[256,2048]{1,0:T(8,128)(2,1)S(1)} collective-permute-done((bf16[256,2048]{1,0:T(8,128)(2,1)S(1)}, bf16[256,2048]{1,0:T(8,128)(2,1)S(1)}, u32[]{:S(2)}, u32[]{:S(2)}) %collective-permute-start.1) | collective-permute-done | bytes 1048608 | tf_op jit(solution)/shard_map/ppermute | solution.py:18
  54.7 4.8 copy.43
  65.1 23.9 %collective-permute-done.2 = bf16[512,2048]{1,0:T(8,128)(2,1)} collective-permute-done((bf16[512,2048]{1,0:T(8,128)(2,1)}, bf16[512,2048]{1,0:T(8,128)(2,1)}, u32[]{:S(2)}, u32[]{:S(2)}) %collective-permute-start.2) | collective-permute-done | bytes 2097184 | tf_op jit(solution)/shard_map/ppermute | solution.py:18
  89.0 7.9 fusion.32
  123.4 101.7 %while.10 = (s32[]{:T(128)}, bf16[2,512,2,128]{3,2,1,0:T(2,128)(2,1)}, pred[5120]{0:T(1024)(128)(4,1)S(1)}, s32[2,512]{1,0:T(2,128)S(1)}, s32[5120]{0:T(1024)S(1...) while((s32[]{:T(128)}, ...), condition=%wide.region_6.7_spmd, body=%wide.region_3.6_spmd.sunk | while | flops 2742167552 | bytes 99685544 | solution.py:113
  127.2 10.3 %fusion.85 = f32[2,512,5120]{2,1,0:T(8,128)} fusion(bf16[5120,2,128]{2,0,1:T(8,128)(2,1)} %get-tuple-element.178, bf16[2,512,2,128]{3,1,2,0:T(8,128)(2,1)S(1)} %get-tuple-element.177, s32[]{:T(128)S(6)} %copy.103), kind=kOutput, calls=%fused_computation.20.clone.1 | convolution fusion | flops 1342177280 | bytes 23855108 | tf_op jit(solution)/shard_map/while/body/eval_jaxpr/nhe,mhe->hnm/dot_general | solution.py:46
  137.6 25.0 %fusion.87 = (f32[2,512]{1,0:T(2,128)S(1)}, f32[2,512,5120]{2,1,0:T(8,128)}) fusion(f32[2,512,5120]{2,1,0:T(8,128)} %fusion.85, pred[512,5120]{1,0:T(8,128)(4,1)S(1)} %fusion.86), kind=kOutput, calls=%fused_computation.123.clone.1 | output fusion | flops 31462400 | bytes 44568576 | tf_op jit(solution)/shard_map/while/body/eval_jaxpr/sub | solution.py:55
  162.5 10.7 %fusion.88 = bf16[1,512,2,128]{3,1,2,0:T(8,128)(2,1)S(1)} fusion(bf16[5120,2,128]{2,0,1:T(8,128)(2,1)} %get-tuple-element.179, f32[2,512,5120]{2,1,0:T(8,128)} %get-tuple-element.152, f32[2,512]{1,0:T(2,128)S(1)} %get-tuple-element.153), kind=kOutput, calls=%fused_computation.18.clone.1 | convolution fusion | flops 1352794112 | bytes 23859200 | tf_op jit(solution)/shard_map/while/body/eval_jaxpr/hnm,mhe->nhe/dot_general | solution.py:57
  177.9 10.3 %fusion.85 = f32[2,512,5120]{2,1,0:T(8,128)} fusion(bf16[5120,2,128]{2,0,1:T(8,128)(2,1)} %get-tuple-element.178, bf16[2,512,2,128]{3,1,2,0:T(8,128)(2,1)S(1)} %get-tuple-element.177, s32[]{:T(128)S(6)} %copy.103), kind=kOutput, calls=%fused_computation.20.clone.1 | convolution fusion | flops 1342177280 | bytes 23855108 | tf_op jit(solution)/shard_map/while/body/eval_jaxpr/nhe,mhe->hnm/dot_general | solution.py:46
  188.3 25.0 %fusion.87 = (f32[2,512]{1,0:T(2,128)S(1)}, f32[2,512,5120]{2,1,0:T(8,128)}) fusion(f32[2,512,5120]{2,1,0:T(8,128)} %fusion.85, pred[512,5120]{1,0:T(8,128)(4,1)S(1)} %fusion.86), kind=kOutput, calls=%fused_computation.123.clone.1 | output fusion | flops 31462400 | bytes 44568576 | tf_op jit(solution)/shard_map/while/body/eval_jaxpr/sub | solution.py:55
  213.3 10.7 %fusion.88 = bf16[1,512,2,128]{3,1,2,0:T(8,128)(2,1)S(1)} fusion(bf16[5120,2,128]{2,0,1:T(8,128)(2,1)} %get-tuple-element.179, f32[2,512,5120]{2,1,0:T(8,128)} %get-tuple-element.152, f32[2,512]{1,0:T(2,128)S(1)} %get-tuple-element.153), kind=kOutput, calls=%fused_computation.18.clone.1 | convolution fusion | flops 1352794112 | bytes 23859200 | tf_op jit(solution)/shard_map/while/body/eval_jaxpr/hnm,mhe->nhe/dot_general | solution.py:57
  236.2 45.9 %reduce-scatter.2.cloned.1.call-done = bf16[128,2048]{1,0:T(8,128)(2,1)} async-done(((bf16[1024,2048]{1,0:T(8,128)(2,1)}), bf16[128,2048]{1,0:T(8,128)(2,1)}) %reduce-scatter.2.cloned.1.call-update) | async-done | bytes 524304 | tf_op jit(solution)/shard_map/reduce_scatter | solution.py:116
  284.7 6.1 gather_fusion
  290.7 6.8 broadcast_in_dim.43
  297.5 188.2 %all_to_all.10 = bf16[32,4,16,2048]{3,2,1,0:T(8,128)(2,1)} all-to-all(bf16[32,4,16,2048]{3,2,1,0:T(8,128)(2,1)} %bitcast.105), channel_id=1, replica_groups=mesh['row'=4,'col'=8] {'row','col'}, dimensions={0} | all-to-all | bytes 16777216 | tf_op jit(solution)/shard_map/all_to_all | solution.py:143
  485.7 21.2 %fusion.22 = f32[32,4,16,1408]{3,2,0,1:T(8,128)} fusion(bf16[4,2048,1408]{2,1,0:T(8,128)(2,1)} %param.26, bf16[32,4,16,2048]{3,2,1,0:T(8,128)(2,1)} %all_to_all.10), kind=kOutput, calls=%fused_computation.35 | convolution fusion | flops 11811160064 | bytes 42991616 | tf_op jit(solution)/shard_map/shcd,hdf->shcf/dot_general | solution.py:141
  506.9 15.5 %convert_bitcast_fusion = bf16[32,4,16,2048]{3,2,0,1:T(8,128)(2,1)} fusion(bf16[4,704,2048]{2,1,0:T(8,128)(2,1)} %param.27, f32[32,4,16,1408]{3,2,0,1:T(8,128)} %fusion.22), kind=kOutput, calls=%fused_computation.34 | convolution fusion | flops 5918425088 | bytes 32505856 | tf_op jit(solution)/shard_map/shcf,hfd->shcd/dot_general | solution.py:150
  522.4 8.3 %copy.57 = bf16[32,4,16,2048]{3,2,1,0:T(8,128)(2,1)} copy(bf16[32,4,16,2048]{3,2,0,1:T(8,128)(2,1)} %convert_bitcast_fusion) | data formatting | bytes 16777216 | tf_op jit(solution)/shard_map/convert_element_type | solution.py:152
  538.7 182.0 %all-to-all-done.1 = bf16[32,4,16,2048]{3,2,1,0:T(8,128)(2,1)} async-done(((bf16[32,4,16,2048]{3,2,1,0:T(8,128)(2,1)}), bf16[32,4,16,2048]{3,2,1,0:T(8,128)(2,1)}, u32[]{:S(2)}, u32[]{:S(2)}) %all-to-all-start.1) | async-done | bytes 8388640 | tf_op jit(solution)/shard_map/all_to_all | solution.py:151
  720.7 11.2 %bitcast_convert_fusion = f32[2048,2048]{1,0:T(8,128)} fusion(bf16[32,4,16,2048]{3,2,1,0:T(8,128)(2,1)} %all-to-all-done.1), kind=kLoop, calls=%fused_computation.32 | loop fusion | flops 4194304 | bytes 25165824 | tf_op jit(solution)/shard_map/reshape | solution.py:154
  731.9 18.3 %gather_fusion.1 = f32[1536,2048]{1,0:T(8,128)} fusion(f32[2048,2048]{1,0:T(8,128)} %bitcast_convert_fusion, s32[2048]{0:T(1024)S(1)} %pad_clamp_fusion), kind=kCustom, calls=%fused_computation.1 | custom fusion | bytes 25171968 | tf_op jit(solution)/shard_map/gather | solution.py:157
  750.2 15.3 %reshape.296 = f32[128,6,2,2048]{3,2,1,0:T(2,128)} reshape(f32[1536,2048]{1,0:T(8,128)} %gather_fusion.1) | data formatting | bytes 25165824 | tf_op jit(solution)/shard_map/reshape | solution.py:157
  765.5 15.6 %fusion.69 = (f32[128,6,1,2048]{3,2,1,0:T(1,128)S(1)}, f32[128,6,1,2048]{3,2,1,0:T(1,128)S(1)}) fusion(f32[128,6,2,2048]{3,2,1,0:T(2,128)} %reshape.296), kind=kLoop, calls=%fused_computation.124 | loop fusion | bytes 25165824 | tf_op jit(solution)/shard_map/slice | solution.py:158
  781.0 7.2 fusion.42
  (117 shorter events, 90.9 us)
Async XLA Ops:
  7.2 217.9 %copy-start = (bf16[256,2048]{1,0:T(8,128)(2,1)S(1)}, bf16[256,2048]{1,0:T(8,128)(2,1)}, u32[]{:S(2)}) copy-start(bf16[256,2048]{1,0:T(8,128)(2,1)} %param.22) | copy-start | bytes 3145732
  7.2 274.8 %reduce-scatter.2.cloned.1.call-start = ((), (), s32[]{:S(2)}) async-start(), calls=%async_computation.3 | async-start | bytes 4718592 | tf_op jit(solution)/shard_map/reduce_scatter | solution.py:116
  10.5 2.1 collective-permute-start
  12.8 26.4 %collective-permute-start.1 = (bf16[256,2048]{1,0:T(8,128)(2,1)S(1)}, bf16[256,2048]{1,0:T(8,128)(2,1)S(1)}, u32[]{:S(2)}, u32[]{:S(2)}) collective-permute-start(bf16[256,2048]{1,0:T(8,128)(2,1)S(1)} %maximum_select_fusion.2), channel_id=1, source_target_pairs={{0,2},{1,3},{2,0},{3,1},{4,6},{5,7},{6,4},{7,5},{8,10},{9,11},{10,... | collective-permute-start | bytes 3145736 | tf_op jit(solution)/shard_map/ppermute | solution.py:18
  41.6 47.5 %collective-permute-start.2 = (bf16[512,2048]{1,0:T(8,128)(2,1)}, bf16[512,2048]{1,0:T(8,128)(2,1)}, u32[]{:S(2)}, u32[]{:S(2)}) collective-permute-start(bf16[512,2048]{1,0:T(8,128)(2,1)} %maximum_select_fusion.1), channel_id=1, source_target_pairs={{0,4},{1,5},{2,6},{3,7},{4,0},{5,1},{6,2},{7,3},{8,12},{9,13},{10,... | collective-permute-start | bytes 6291464 | tf_op jit(solution)/shard_map/ppermute | solution.py:18
  50.4 9.0 %copy-start.14 = (s32[4]{0:T(128)S(1)}, s32[4]{0:T(128)}, u32[]{:S(2)}) copy-start(s32[4]{0:T(128)} %param.17) | copy-start | bytes 52
  50.4 9.7 %copy-start.15 = (s32[4]{0:T(128)S(1)}, s32[4]{0:T(128)}, u32[]{:S(2)}) copy-start(s32[4]{0:T(128)} %param.16) | copy-start | bytes 52
  96.9 1.7 copy-start.6
  96.9 3.1 copy-start.2
  116.1 0.8 copy-start.3
  118.6 4.5 copy-start.7
  118.6 4.5 copy-start.8
  162.5 10.7 %copy-start.9 = (bf16[2,512,2,128]{3,2,1,0:T(2,128)(2,1)S(1)}, bf16[2,512,2,128]{3,2,1,0:T(2,128)(2,1)}, u32[]{:S(2)}) copy-start(bf16[2,512,2,128]{3,2,1,0:T(2,128)(2,1)} %get-tuple-element.164) | copy-start | bytes 1572868 | tf_op jit(solution)/shard_map/while
  173.5 0.8 copy-start.10
  213.3 10.7 %copy-start.9 = (bf16[2,512,2,128]{3,2,1,0:T(2,128)(2,1)S(1)}, bf16[2,512,2,128]{3,2,1,0:T(2,128)(2,1)}, u32[]{:S(2)}) copy-start(bf16[2,512,2,128]{3,2,1,0:T(2,128)(2,1)} %get-tuple-element.164) | copy-start | bytes 1572868 | tf_op jit(solution)/shard_map/while
  224.3 0.8 copy-start.10
  225.1 4.3 copy-start.11
  225.1 4.7 copy-start.12
  225.1 57.0 %copy-start.1 = (bf16[128,2048]{1,0:T(8,128)(2,1)S(1)}, bf16[128,2048]{1,0:T(8,128)(2,1)}, u32[]{:S(2)}) copy-start(bf16[128,2048]{1,0:T(8,128)(2,1)} %param.15) | copy-start | bytes 1572868
  530.6 4.0 copy-start.13
  530.6 7.0 copy-start.4
  530.6 190.0 %all-to-all-start.1 = ((bf16[32,4,16,2048]{3,2,1,0:T(8,128)(2,1)}), bf16[32,4,16,2048]{3,2,1,0:T(8,128)(2,1)}, u32[]{:S(2)}, u32[]{:S(2)}) async-start(bf16[32,4,16,2048]{3,2,1,0:T(8,128)(2,1)} %copy.57), calls=%async_computation.2 | async-start | bytes 16777216 | tf_op jit(solution)/shard_map/all_to_all | solution.py:151
  788.2 2.6 copy-start.5
Sparse Core Ops, SparseCore 0:
  229.5 52.4 reduce-scatter.1
